TPU v7x, 32 devices: a whole 2x2x4 slice. The times are simulated.
32 devices in a mesh: gx: 4 (over y, x), gy: 2 (over core), gz: 4 (over z).
Axes of the slice: x: 2, y: 2, z: 4, core: 2. Of those that a mesh axis runs over, the one named last changes fastest.
Arguments:
- load_vector: float32 [32, 32, 2048], P(('gx', 'gy', 'gz')), may hold values from -24 to 24
- matrix_tiles: float32 [512, 7, 128, 128], P(('gx', 'gy', 'gz')), may hold values from -1 to 6, as said below
- tile_cols: int32 [512, 7], P(('gx', 'gy', 'gz')), may hold values from 0 to 15, as said below
- interior_inv: float32 [384, 128, 128], P(('gx', 'gy', 'gz')), may hold values from -0.1 to 0.3, as said below
- schur_inv: float32 [32, 512, 512], P(('gx', 'gy', 'gz')), may hold values from -0.1 to 0.3, as said below
- coarse_basis: float32 [32, 128, 2048], P(('gx', 'gy', 'gz')), may hold values from -0.125 to 0.125
- coarse_inv: float32 [32, 256, 256], P(('gx', 'gy', 'gz')), may hold values from -0.2 to 0.8, as said below
- row_map: int32 [32, 4, 128], P(('gx', 'gy', 'gz')), may hold values from 0 to 127, each once within a row
- face_link: int32 [32, 4], P(('gx', 'gy', 'gz')), may hold values from 0 to 1, as said below
- coarse_id: int32 [32, 4], P(('gx', 'gy', 'gz')), may hold values from 0 to 31, as said below
Outputs:
- solution: float32 [32, 32, 2048], P(('gx', 'gy', 'gz'))
- residual: float32 [32, 32, 2048], P(('gx', 'gy', 'gz'))
Inputs may be any that keep to these rules, and one draw needn't show every extreme that they name: `matrix_tiles`: tile 0 of each block row is its diagonal tile; each subdomain's matrix is symmetric positive definite: the tile of block row i in column block j is the transpose of the tile of block row j in column block i. `tile_cols`: tile 0 of block row i sits in column block i; tiles 1 to 6 sit in column blocks i + a, i - a, i + b, i - b, i + c, i - c modulo 16, for three distinct offsets a, b, c of that subdomain between 1 and (15) // 2; every column block holds exactly 7 tiles. `interior_inv`: each block is symmetric positive definite. `schur_inv`: symmetric positive definite. `coarse_inv`: symmetric positive definite. For partners d and e of round r, entry k of row_map[d, r] and of row_map[e, r] name the same shared unknown. `face_link`: equal for the two partners of a round. coarse_id = owner * 8 + slot, owner being a gz index within the subdomain's line of 4 devices; blocks with the same target are summed. Each subdomain sends at most 2 blocks to one owner and exactly 2 to some owner.
All inputs are finite; a program needn't handle non-finite values.
Results may differ from a plain program's by a relative error of at most 0.00018.
Values sent between devices are 32-bit elements; how exact they have to be, the bound alone decides.
No kernel may reach another device: no remote copies, remote signals or barrier semaphores. Data moves between devices by JAX's collectives and lax.ppermute only.
A program may use at most 64 MiB of HBM per device.

v0:
```python
import jax
import jax.numpy as jnp
from jax import lax
from jax.sharding import PartitionSpec as P

BS = 128
NIN = 12
NRHS = 32
CW = 32
CB = 4
OCAP = 8
ITERS = 2
NB = 16
NL = 2048
HIGH = lax.Precision.HIGHEST


def partner(value, axis, distance):
    return lax.ppermute(value, axis, [(i, i ^ 1 << distance) for i in range(lax.axis_size(axis))])


def on_device(
    load_vector,
    matrix_tiles,
    tile_cols,
    interior_inv,
    schur_inv,
    coarse_basis,
    coarse_inv,
    row_map,
    face_link,
    coarse_id,
):
    load_rows = load_vector[0]
    link_vals = face_link[0]
    face_maps = row_map[0]
    basis_rows = coarse_basis[0]
    schur_mat = schur_inv[0]
    coarse_mat = coarse_inv[0]
    block_ids = coarse_id[0]
    offset = NIN * BS
    line_size = lax.axis_size("gz")
    depth_z = line_size.bit_length() - 1
    depth_y = lax.axis_size("gy").bit_length() - 1
    swap_bits = [0, 1, depth_z, depth_z + depth_y]
    link_float = link_vals.astype(jnp.float32)
    weight = jnp.concatenate(
        [jnp.ones((offset,), jnp.float32)]
        + [jnp.broadcast_to(1.0 - 0.5 * link_float[round_no], (BS,)) for round_no in range(4)]
    )
    lane_ids = jnp.arange(BS, dtype=jnp.int32)
    onehots = [
        (face_maps[round_no][:, None] == lane_ids[None, :]).astype(jnp.float32)
        for round_no in range(4)
    ]

    def assemble(vector):
        outgoing = []
        for round_no in range(4):
            face_rows = vector[:, offset + round_no * BS : offset + (round_no + 1) * BS]
            outgoing.append(jnp.einsum("nj,kj->nk", face_rows, onehots[round_no], precision=HIGH))
        pieces = [vector[:, :offset]]
        for round_no in range(4):
            incoming = partner(outgoing[round_no], ("gx", "gy", "gz"), swap_bits[round_no])
            returned = jnp.dot(incoming, onehots[round_no], precision=HIGH)
            face_rows = vector[:, offset + round_no * BS : offset + (round_no + 1) * BS]
            pieces.append(face_rows + link_float[round_no] * returned)
        return jnp.concatenate(pieces, axis=1)

    group_rows = jnp.arange(line_size * OCAP, dtype=jnp.int32)
    dense_map = (group_rows[:, None] == block_ids[None, :]).astype(jnp.float32)

    def coarse_solve(summed):
        flat_rows = summed.reshape(OCAP * CW, NRHS)
        return jnp.dot(coarse_mat, flat_rows, precision=HIGH).reshape(OCAP, CW * NRHS)

    def coarse_part(contrib):
        summed = lax.psum_scatter(
            jnp.dot(dense_map, contrib, precision=HIGH), "gz", scatter_dimension=0, tiled=True
        )
        solved = coarse_solve(summed)
        all_solved = lax.all_gather(solved, "gz", axis=0, tiled=True)
        return jnp.einsum("ab,ac->bc", dense_map, all_solved, precision=HIGH)

    def precondition(resid):
        scaled = weight * resid
        inner_part = jnp.einsum(
            "bij,nbj->nbi", interior_inv, scaled[:, :offset].reshape(NRHS, NIN, BS), precision=HIGH
        ).reshape(NRHS, offset)
        outer_part = jnp.einsum("ij,nj->ni", schur_mat, scaled[:, offset:], precision=HIGH)
        contrib = jnp.einsum("cl,nl->cn", basis_rows, scaled, precision=HIGH).reshape(CB, CW * NRHS)
        coarse_back = coarse_part(contrib).reshape(CB * CW, NRHS)
        correction = jnp.einsum("cn,cl->nl", coarse_back, basis_rows, precision=HIGH)
        return assemble(weight * (jnp.concatenate([inner_part, outer_part], axis=1) + correction))

    def local_dot(left, right):
        return jnp.sum(weight * left * right, axis=1)

    resid = assemble(load_rows)
    solution = jnp.zeros_like(resid)
    precond_res = precondition(resid)

    def global_rz(left, right):
        return lax.psum(local_dot(left, right), ("gx", "gy", "gz"))

    direction = precond_res
    rho_now = global_rz(resid, precond_res)
    for turn_no in range(ITERS):
        picked = direction.reshape(NRHS, NB, BS)[:, tile_cols]
        product = jnp.einsum("rtij,nrtj->nri", matrix_tiles, picked, precision=HIGH).reshape(
            NRHS, NL
        )
        product_dir = assemble(product)
        curve_sum = lax.psum(local_dot(direction, product_dir), ("gx", "gy", "gz"))
        step_len = (rho_now / curve_sum)[:, None]
        solution = solution + step_len * direction
        resid = resid - step_len * product_dir
        if turn_no + 1 < ITERS:
            precond_res = precondition(resid)
            rho_next = global_rz(resid, precond_res)
            direction = precond_res + (rho_next / rho_now)[:, None] * direction
            rho_now = rho_next
    return (solution[None], resid[None])


def solution(mesh):
    in_specs = (
        P(("gx", "gy", "gz"), None, None),
        P(("gx", "gy", "gz"), None, None, None),
        P(("gx", "gy", "gz"), None),
        P(("gx", "gy", "gz"), None, None),
        P(("gx", "gy", "gz"), None, None),
        P(("gx", "gy", "gz"), None, None),
        P(("gx", "gy", "gz"), None, None),
        P(("gx", "gy", "gz"), None, None),
        P(("gx", "gy", "gz"), None),
        P(("gx", "gy", "gz"), None),
    )
    out_specs = (P(("gx", "gy", "gz"), None, None), P(("gx", "gy", "gz"), None, None))
    return jax.shard_map(
        on_device, mesh=mesh, in_specs=in_specs, out_specs=out_specs, check_vma=False
    )
```

profile of v0, /device:TPU:0, one launch (start us, length us, event | category | flops | bytes accessed | tf_op | source)
XLA Modules:
  0.0 299.2 jit_solution(18162430448153305590)
XLA Ops:
  9.0 3.1 %collective-permute-start = (f32[32,128]{0,1:T(8,128)S(1)}, f32[32,128]{0,1:T(8,128)S(1)}, u32[]{:S(2)}, u32[]{:S(2)}) collective-permute-start(f32[32,128]{0,1:T(8,128)S(1)} %convolution_bitcast_fusion.7), channel_id=1, source_target_pairs={{0,1},{1,0},{2,3},{3,2},{4,5},{5,4},{6,7},{7,6},{8,9},{9,8},{10,11... | collective-permute-start | bytes 49160 | tf_op jit(solution)/shard_map/ppermute | solution.py:19
  13.1 2.7 collective-permute-start.1
  17.7 1.6 collective-permute-start.3
  20.2 1.6 bitcast_dynamic-update-slice_fusion.2
  26.6 1.5 constant_dynamic-update-slice_fusion.4
  28.2 1.7 constant_dynamic-update-slice_fusion.3
  29.9 1.6 constant_dynamic-update-slice_fusion.2
  31.5 2.2 constant_dynamic-update-slice_fusion.1
  35.8 1.5 fusion.97
  41.6 12.3 %reduce-scatter.3.cloned.1.call-done = f32[8,1024]{1,0:T(8,128)} async-done(((f32[32,1024]{1,0:T(8,128)}), f32[8,1024]{1,0:T(8,128)}) %reduce-scatter.3.cloned.1.call-update) | async-done | bytes 32784 | tf_op jit(solution)/shard_map/reduce_scatter | solution.py:78
  55.3 13.4 %all_gather.6 = f32[32,1024]{1,0:T(8,128)S(1)} all-gather(f32[8,1024]{1,0:T(8,128)S(1)} %reshape.579), channel_id=1, replica_groups=mesh['gx'=4,'gy'=2,'gz'=4] {'gz'}, dimensions={0}, use_global_device_ids=true | all-gather | bytes 163840 | tf_op jit(solution)/shard_map/all_gather | solution.py:82
  79.5 9.9 %convolution_bitcast_fusion.1 = f32[16,4,8,128]{3,2,1,0:T(8,128)S(1)} fusion(f32[32,16,7,128]{3,0,2,1:T(8,128)S(1)} %bitcast.200, f32[16,7,128,128]{3,2,1,0:T(8,128)} %param.11), kind=kOutput, calls=%fused_computation.7 | convolution fusion | flops 704643072 | bytes 9437184 | tf_op jit(solution)/shard_map/rtij,nrtj->nri/dot_general | solution.py:110
  91.2 2.0 collective-permute-start.8
  94.0 1.6 collective-permute-start.11
  102.3 39.3 %all-reduce = (f32[32]{0:T(128)S(1)}, f32[32]{0:T(128)S(1)}) all-reduce(f32[32]{0:T(128)S(1)} %get-tuple-element.3, f32[32]{0:T(128)S(1)} %get-tuple-element.2), channel_id=1, replica_groups=mesh['gx'=4,'gy'=2,'gz'=4] {'gx','gy','gz'}, use_global_device_ids=true, to_apply=%region_2.0 | all-reduce | flops 64 | bytes 512 | tf_op jit(solution)/shard_map/psum | solution.py:104
  144.2 1.5 fusion.95
  151.3 14.2 %reduce-scatter.5.cloned.1.call-done = f32[8,1024]{1,0:T(8,128)} async-done(((f32[32,1024]{1,0:T(8,128)}), f32[8,1024]{1,0:T(8,128)}) %reduce-scatter.5.cloned.1.call-update) | async-done | bytes 32784 | tf_op jit(solution)/shard_map/reduce_scatter | solution.py:78
  167.0 13.3 %all_gather.7 = f32[32,1024]{1,0:T(8,128)S(1)} all-gather(f32[8,1024]{1,0:T(8,128)S(1)} %reshape.587), channel_id=1, replica_groups=mesh['gx'=4,'gy'=2,'gz'=4] {'gz'}, dimensions={0}, use_global_device_ids=true | all-gather | bytes 163840 | tf_op jit(solution)/shard_map/all_gather | solution.py:82
  183.6 1.5 collective-permute-start.15
  190.5 40.7 %psum.30 = f32[32]{0:T(128)S(1)} all-reduce(f32[32]{0:T(128)S(1)} %multiply_reduce_fusion.1), channel_id=1, replica_groups=mesh['gx'=4,'gy'=2,'gz'=4] {'gx','gy','gz'}, use_global_device_ids=true, to_apply=%region_7.0 | all-reduce | flops 32 | bytes 256 | tf_op jit(solution)/shard_map/psum | solution.py:104
  232.0 9.9 %convolution_bitcast_fusion = f32[16,4,8,128]{3,2,1,0:T(8,128)S(1)} fusion(f32[32,16,7,128]{3,0,2,1:T(8,128)S(1)} %bitcast.199, f32[16,7,128,128]{3,2,1,0:T(8,128)} %param.11), kind=kOutput, calls=%fused_computation.6 | convolution fusion | flops 704643072 | bytes 9437184 | tf_op jit(solution)/shard_map/rtij,nrtj->nri/dot_general | solution.py:110
  243.2 2.1 collective-permute-start.17
  245.3 2.3 collective-permute-start.19
  251.3 40.0 %psum.31 = f32[32]{0:T(128)S(1)} all-reduce(f32[32]{0:T(128)S(1)} %multiply_reduce_fusion), channel_id=1, replica_groups=mesh['gx'=4,'gy'=2,'gz'=4] {'gx','gy','gz'}, use_global_device_ids=true, to_apply=%region_9.0 | all-reduce | flops 32 | bytes 256 | tf_op jit(solution)/shard_map/psum | solution.py:114
  (222 shorter events, 60.1 us)
Async XLA Ops:
  7.2 46.7 %reduce-scatter.3.cloned.1.call-start = ((), (), s32[]{:S(2)}) async-start(), calls=%async_computation.2 | async-start | bytes 163840 | tf_op jit(solution)/shard_map/reduce_scatter | solution.py:78
  9.0 17.6 %collective-permute-start = (f32[32,128]{0,1:T(8,128)S(1)}, f32[32,128]{0,1:T(8,128)S(1)}, u32[]{:S(2)}, u32[]{:S(2)}) collective-permute-start(f32[32,128]{0,1:T(8,128)S(1)} %convolution_bitcast_fusion.7), channel_id=1, source_target_pairs={{0,1},{1,0},{2,3},{3,2},{4,5},{5,4},{6,7},{7,6},{8,9},{9,8},{10,11... | collective-permute-start | bytes 49160 | tf_op jit(solution)/shard_map/ppermute | solution.py:19
  13.1 15.1 %collective-permute-start.1 = (f32[32,128]{0,1:T(8,128)S(1)}, f32[32,128]{0,1:T(8,128)S(1)}, u32[]{:S(2)}, u32[]{:S(2)}) collective-permute-start(f32[32,128]{0,1:T(8,128)S(1)} %convolution_bitcast_fusion.6), channel_id=1, source_target_pairs={{0,2},{1,3},{2,0},{3,1},{4,6},{5,7},{6,4},{7,5},{8,10},{9,11},{10,... | collective-permute-start | bytes 49160 | tf_op jit(solution)/shard_map/ppermute | solution.py:19
  16.7 13.2 %collective-permute-start.2 = (f32[32,128]{0,1:T(8,128)S(1)}, f32[32,128]{0,1:T(8,128)S(1)}, u32[]{:S(2)}, u32[]{:S(2)}) collective-permute-start(f32[32,128]{0,1:T(8,128)S(1)} %convolution_bitcast_fusion.5), channel_id=1, source_target_pairs={{0,4},{1,5},{2,6},{3,7},{4,0},{5,1},{6,2},{7,3},{8,12},{9,13},{10,... | collective-permute-start | bytes 49160 | tf_op jit(solution)/shard_map/ppermute | solution.py:19
  17.7 13.7 %collective-permute-start.3 = (f32[32,128]{0,1:T(8,128)S(1)}, f32[32,128]{0,1:T(8,128)S(1)}, u32[]{:S(2)}, u32[]{:S(2)}) collective-permute-start(f32[32,128]{0,1:T(8,128)S(1)} %convolution_bitcast_fusion.4), channel_id=1, source_target_pairs={{0,8},{1,9},{2,10},{3,11},{4,12},{5,13},{6,14},{7,15},{8,0},{9,1},... | collective-permute-start | bytes 49160 | tf_op jit(solution)/shard_map/ppermute | solution.py:19
  37.3 128.2 %reduce-scatter.5.cloned.1.call-start = ((), (), s32[]{:S(2)}) async-start(), calls=%async_computation.3 | async-start | bytes 163840 | tf_op jit(solution)/shard_map/reduce_scatter | solution.py:78
  71.2 3.7 %collective-permute-start.4 = (f32[32,128]{1,0:T(8,128)S(1)}, f32[32,128]{1,0:T(8,128)S(1)}, u32[]{:S(2)}, u32[]{:S(2)}) collective-permute-start(f32[32,128]{1,0:T(8,128)S(1)} %fusion.53), channel_id=1, source_target_pairs={{0,1},{1,0},{2,3},{3,2},{4,5},{5,4},{6,7},{7,6},{8,9},{9,8},{10,11... | collective-permute-start | bytes 49160 | tf_op jit(solution)/shard_map/ppermute | solution.py:19
  71.4 4.7 %collective-permute-start.5 = (f32[32,128]{1,0:T(8,128)S(1)}, f32[32,128]{1,0:T(8,128)S(1)}, u32[]{:S(2)}, u32[]{:S(2)}) collective-permute-start(f32[32,128]{1,0:T(8,128)S(1)} %fusion.49), channel_id=1, source_target_pairs={{0,2},{1,3},{2,0},{3,1},{4,6},{5,7},{6,4},{7,5},{8,10},{9,11},{10,... | collective-permute-start | bytes 49160 | tf_op jit(solution)/shard_map/ppermute | solution.py:19
  72.7 4.3 %collective-permute-start.6 = (f32[32,128]{1,0:T(8,128)S(1)}, f32[32,128]{1,0:T(8,128)S(1)}, u32[]{:S(2)}, u32[]{:S(2)}) collective-permute-start(f32[32,128]{1,0:T(8,128)S(1)} %fusion.45), channel_id=1, source_target_pairs={{0,4},{1,5},{2,6},{3,7},{4,0},{5,1},{6,2},{7,3},{8,12},{9,13},{10,... | collective-permute-start | bytes 49160 | tf_op jit(solution)/shard_map/ppermute | solution.py:19
  72.7 5.2 %collective-permute-start.7 = (f32[32,128]{1,0:T(8,128)S(1)}, f32[32,128]{1,0:T(8,128)S(1)}, u32[]{:S(2)}, u32[]{:S(2)}) collective-permute-start(f32[32,128]{1,0:T(8,128)S(1)} %fusion.41), channel_id=1, source_target_pairs={{0,8},{1,9},{2,10},{3,11},{4,12},{5,13},{6,14},{7,15},{8,0},{9,1},... | collective-permute-start | bytes 49160 | tf_op jit(solution)/shard_map/ppermute | solution.py:19
  91.2 6.8 %collective-permute-start.8 = (f32[32,128]{1,0:T(8,128)S(1)}, f32[32,128]{1,0:T(8,128)S(1)}, u32[]{:S(2)}, u32[]{:S(2)}) collective-permute-start(f32[32,128]{1,0:T(8,128)S(1)} %fusion.52), channel_id=1, source_target_pairs={{0,1},{1,0},{2,3},{3,2},{4,5},{5,4},{6,7},{7,6},{8,9},{9,8},{10,11... | collective-permute-start | bytes 49160 | tf_op jit(solution)/shard_map/ppermute | solution.py:19
  93.2 5.6 %collective-permute-start.9 = (f32[32,128]{1,0:T(8,128)S(1)}, f32[32,128]{1,0:T(8,128)S(1)}, u32[]{:S(2)}, u32[]{:S(2)}) collective-permute-start(f32[32,128]{1,0:T(8,128)S(1)} %fusion.48), channel_id=1, source_target_pairs={{0,2},{1,3},{2,0},{3,1},{4,6},{5,7},{6,4},{7,5},{8,10},{9,11},{10,... | collective-permute-start | bytes 49160 | tf_op jit(solution)/shard_map/ppermute | solution.py:19
  94.0 5.7 %collective-permute-start.10 = (f32[32,128]{1,0:T(8,128)S(1)}, f32[32,128]{1,0:T(8,128)S(1)}, u32[]{:S(2)}, u32[]{:S(2)}) collective-permute-start(f32[32,128]{1,0:T(8,128)S(1)} %fusion.44), channel_id=1, source_target_pairs={{0,4},{1,5},{2,6},{3,7},{4,0},{5,1},{6,2},{7,3},{8,12},{9,13},{10,... | collective-permute-start | bytes 49160 | tf_op jit(solution)/shard_map/ppermute | solution.py:19
  94.0 6.7 %collective-permute-start.11 = (f32[32,128]{1,0:T(8,128)S(1)}, f32[32,128]{1,0:T(8,128)S(1)}, u32[]{:S(2)}, u32[]{:S(2)}) collective-permute-start(f32[32,128]{1,0:T(8,128)S(1)} %fusion.40), channel_id=1, source_target_pairs={{0,8},{1,9},{2,10},{3,11},{4,12},{5,13},{6,14},{7,15},{8,0},{9,1},... | collective-permute-start | bytes 49160 | tf_op jit(solution)/shard_map/ppermute | solution.py:19
  180.3 50.8 %copy-start.31 = (f32[32]{0:T(128)S(1)}, f32[32]{0:T(128)}, u32[]{:S(2)}) copy-start(f32[32]{0:T(128)} %copy-done.30) | copy-start | bytes 388
  182.0 3.8 %collective-permute-start.12 = (f32[32,128]{1,0:T(8,128)S(1)}, f32[32,128]{1,0:T(8,128)S(1)}, u32[]{:S(2)}, u32[]{:S(2)}) collective-permute-start(f32[32,128]{1,0:T(8,128)S(1)} %fusion.51), channel_id=1, source_target_pairs={{0,1},{1,0},{2,3},{3,2},{4,5},{5,4},{6,7},{7,6},{8,9},{9,8},{10,11... | collective-permute-start | bytes 49160 | tf_op jit(solution)/shard_map/ppermute | solution.py:19
  182.3 4.7 %collective-permute-start.13 = (f32[32,128]{1,0:T(8,128)S(1)}, f32[32,128]{1,0:T(8,128)S(1)}, u32[]{:S(2)}, u32[]{:S(2)}) collective-permute-start(f32[32,128]{1,0:T(8,128)S(1)} %fusion.47), channel_id=1, source_target_pairs={{0,2},{1,3},{2,0},{3,1},{4,6},{5,7},{6,4},{7,5},{8,10},{9,11},{10,... | collective-permute-start | bytes 49160 | tf_op jit(solution)/shard_map/ppermute | solution.py:19
  183.6 4.3 %collective-permute-start.14 = (f32[32,128]{1,0:T(8,128)S(1)}, f32[32,128]{1,0:T(8,128)S(1)}, u32[]{:S(2)}, u32[]{:S(2)}) collective-permute-start(f32[32,128]{1,0:T(8,128)S(1)} %fusion.43), channel_id=1, source_target_pairs={{0,4},{1,5},{2,6},{3,7},{4,0},{5,1},{6,2},{7,3},{8,12},{9,13},{10,... | collective-permute-start | bytes 49160 | tf_op jit(solution)/shard_map/ppermute | solution.py:19
  183.6 5.2 %collective-permute-start.15 = (f32[32,128]{1,0:T(8,128)S(1)}, f32[32,128]{1,0:T(8,128)S(1)}, u32[]{:S(2)}, u32[]{:S(2)}) collective-permute-start(f32[32,128]{1,0:T(8,128)S(1)} %fusion.39), channel_id=1, source_target_pairs={{0,8},{1,9},{2,10},{3,11},{4,12},{5,13},{6,14},{7,15},{8,0},{9,1},... | collective-permute-start | bytes 49160 | tf_op jit(solution)/shard_map/ppermute | solution.py:19
  242.0 49.3 %copy-start.33 = (f32[32]{0:T(128)S(1)}, f32[32]{0:T(128)}, u32[]{:S(2)}) copy-start(f32[32]{0:T(128)} %copy-done.32) | copy-start | bytes 388
  243.1 4.5 %collective-permute-start.16 = (f32[32,128]{1,0:T(8,128)S(1)}, f32[32,128]{1,0:T(8,128)S(1)}, u32[]{:S(2)}, u32[]{:S(2)}) collective-permute-start(f32[32,128]{1,0:T(8,128)S(1)} %fusion.50), channel_id=1, source_target_pairs={{0,1},{1,0},{2,3},{3,2},{4,5},{5,4},{6,7},{7,6},{8,9},{9,8},{10,11... | collective-permute-start | bytes 49160 | tf_op jit(solution)/shard_map/ppermute | solution.py:19
  243.2 5.2 %collective-permute-start.17 = (f32[32,128]{1,0:T(8,128)S(1)}, f32[32,128]{1,0:T(8,128)S(1)}, u32[]{:S(2)}, u32[]{:S(2)}) collective-permute-start(f32[32,128]{1,0:T(8,128)S(1)} %fusion.46), channel_id=1, source_target_pairs={{0,2},{1,3},{2,0},{3,1},{4,6},{5,7},{6,4},{7,5},{8,10},{9,11},{10,... | collective-permute-start | bytes 49160 | tf_op jit(solution)/shard_map/ppermute | solution.py:19
  245.3 4.0 %collective-permute-start.18 = (f32[32,128]{1,0:T(8,128)S(1)}, f32[32,128]{1,0:T(8,128)S(1)}, u32[]{:S(2)}, u32[]{:S(2)}) collective-permute-start(f32[32,128]{1,0:T(8,128)S(1)} %fusion.42), channel_id=1, source_target_pairs={{0,4},{1,5},{2,6},{3,7},{4,0},{5,1},{6,2},{7,3},{8,12},{9,13},{10,... | collective-permute-start | bytes 49160 | tf_op jit(solution)/shard_map/ppermute | solution.py:19
  245.3 4.9 %collective-permute-start.19 = (f32[32,128]{1,0:T(8,128)S(1)}, f32[32,128]{1,0:T(8,128)S(1)}, u32[]{:S(2)}, u32[]{:S(2)}) collective-permute-start(f32[32,128]{1,0:T(8,128)S(1)} %fusion.38), channel_id=1, source_target_pairs={{0,8},{1,9},{2,10},{3,11},{4,12},{5,13},{6,14},{7,15},{8,0},{9,1},... | collective-permute-start | bytes 49160 | tf_op jit(solution)/shard_map/ppermute | solution.py:19
  (32 other events, 767.2 us)
Sparse Core Ops, SparseCore 0:
  37.4 16.4 reduce-scatter.2
  145.9 19.6 reduce-scatter.4
where the time goes:
time: 300 us; the launch traced here: 299 us
  blocking collectives  147 us (49%)
  matrix products  60.6 us (20%)
  waiting for transfers between devices  28.8 us (10%)
  starting transfers between devices  22 us (7%)
  local copies, waits for them, and re-layouts  20.4 us (7%)
  between operations  17.6 us (6%)
  other arithmetic  3.1 us (1%)
    psum x2, blocking collectives, global_rz(): return lax.psum(local_dot(left, right), ('gx', 'gy', 'gz'))  80 us
    psum x1, blocking collectives, on_device(): curve_sum = lax.psum(local_dot(direction, product_dir), ('gx', 'gy', 'gz'))  40 us
    all_gather x2, blocking collectives, coarse_part(): all_solved = lax.all_gather(solved, 'gz', axis=0, tiled=True)  26.7 us
    reduce_scatter x2, waiting for transfers between devices, coarse_part(): lax.psum_scatter(jnp.dot(dense_map, contrib, precision=HIGH), 'gz', scatt...  26.5 us
    ppermute x20, starting transfers between devices, partner(): lax.ppermute(value, axis, [(i, i ^ 1 << distance) for i in range(lax.axis...  21.9 us
    dot_general x20, matrix products, assemble(): returned = jnp.dot(incoming, onehots[round_no], precision=HIGH)  21 us
    dot_general x2, matrix products, on_device(): jnp.einsum('rtij,nrtj->nri', matrix_tiles, picked, precision=HIGH)  19.8 us
    unnamed x97, local copies, waits for them, and re-layouts  12.5 us
  transfers between devices with their start and end apart: 22, of which 6 were waited for; matrix products, arithmetic and copies ran while one was open for 12% of the time, Pallas kernels for 0%

commit v1 on v0

--- a/solution.py
+++ b/solution.py
@@ -2,6 +2,7 @@
 import jax.numpy as jnp
 from jax import lax
 from jax.sharding import PartitionSpec as P
+from jax.lax import axis_index, axis_size, ppermute
 
 BS = 128
 NIN = 12
@@ -79,7 +80,19 @@
             jnp.dot(dense_map, contrib, precision=HIGH), "gz", scatter_dimension=0, tiled=True
         )
         solved = coarse_solve(summed)
-        all_solved = lax.all_gather(solved, "gz", axis=0, tiled=True)
+        block_now = axis_size("gz")
+        everything = axis_index("gz")
+        inter, extra = (block_now, everything)
+        all_solved, view_out = (solved, 1)
+        while view_out < inter:
+            shelf = []
+            for b in range(inter):
+                shelf.append((b, b ^ view_out))
+            current_block = ppermute(all_solved, axis_name="gz", perm=shelf)
+            state_now = jnp.concatenate([all_solved, current_block], axis=0)
+            ready = jnp.concatenate([current_block, all_solved], axis=0)
+            all_solved = jnp.where(extra & view_out == 0, state_now, ready)
+            view_out = 2 * view_out
         return jnp.einsum("ab,ac->bc", dense_map, all_solved, precision=HIGH)
 
     def precondition(resid):

time: 300 us -> 296 us (0.987)
  blocking collectives: 147 us -> 118 us
  waiting for transfers between devices: 28.8 us -> 47.7 us
    all_gather x2 -> x0, blocking collectives: 26.7 us -> none  [coarse_part(): all_solved = lax.all_gather(solved, 'gz', axis=0, tiled=True)]
    ppermute x0 -> x4, waiting for transfers between devices: none -> 13.3 us  [coarse_part(): current_block = ppermute(all_solved, axis_name='gz', perm=shelf)]
    reduce_scatter x2, waiting for transfers between devices: 26.5 us -> 30.7 us  [coarse_part(): lax.psum_scatter(jnp.dot(dense_map, contrib, precision=HIGH), 'gz', scatt...]
    unnamed x97 -> x89, local copies, waits for them, and re-layouts: 12.5 us -> 14.3 us
  transfers between devices with their start and end apart: 22 -> 26, of which waited for: 6 -> 10; matrix products, arithmetic and copies ran while one was open for 12% -> 13% of each run, Pallas kernels for 0% -> 0%
where the time goes in v1:
time: 296 us; the launch traced here: 295 us
  blocking collectives  118 us (40%)
  matrix products  62.4 us (21%)
  waiting for transfers between devices  47.7 us (16%)
  starting transfers between devices  22.3 us (8%)
  local copies, waits for them, and re-layouts  22.1 us (7%)
  between operations  17.6 us (6%)
  other arithmetic  4.07 us (1%)
    psum x2, blocking collectives, global_rz(): return lax.psum(local_dot(left, right), ('gx', 'gy', 'gz'))  80.1 us
    psum x1, blocking collectives, on_device(): curve_sum = lax.psum(local_dot(direction, product_dir), ('gx', 'gy', 'gz'))  38.2 us
    reduce_scatter x2, waiting for transfers between devices, coarse_part(): lax.psum_scatter(jnp.dot(dense_map, contrib, precision=HIGH), 'gz', scatt...  30.7 us
    dot_general x20, matrix products, assemble(): returned = jnp.dot(incoming, onehots[round_no], precision=HIGH)  21 us
    ppermute x20, starting transfers between devices, partner(): lax.ppermute(value, axis, [(i, i ^ 1 << distance) for i in range(lax.axis...  20.1 us
    dot_general x2, matrix products, on_device(): jnp.einsum('rtij,nrtj->nri', matrix_tiles, picked, precision=HIGH)  19.8 us
    unnamed x89, local copies, waits for them, and re-layouts  14.3 us
    ppermute x4, waiting for transfers between devices, coarse_part(): current_block = ppermute(all_solved, axis_name='gz', perm=shelf)  13.3 us
  transfers between devices with their start and end apart: 26, of which 10 were waited for; matrix products, arithmetic and copies ran while one was open for 13% of the time, Pallas kernels for 0%

profile of v1, /device:TPU:0, one launch (start us, length us, event | category | flops | bytes accessed | tf_op | source)
XLA Modules:
  0.0 294.5 jit_solution(14877393049228928822)
XLA Ops:
  9.0 3.1 %collective-permute-start = (f32[32,128]{0,1:T(8,128)S(1)}, f32[32,128]{0,1:T(8,128)S(1)}, u32[]{:S(2)}, u32[]{:S(2)}) collective-permute-start(f32[32,128]{0,1:T(8,128)S(1)} %convolution_bitcast_fusion.7), channel_id=1, source_target_pairs={{0,1},{1,0},{2,3},{3,2},{4,5},{5,4},{6,7},{7,6},{8,9},{9,8},{10,11... | collective-permute-start | bytes 49160 | tf_op jit(solution)/shard_map/ppermute | solution.py:20
  13.1 2.7 collective-permute-start.1
  17.7 1.6 collective-permute-start.3
  20.2 1.6 bitcast_dynamic-update-slice_fusion.2
  26.7 1.5 constant_dynamic-update-slice_fusion.4
  28.2 1.7 constant_dynamic-update-slice_fusion.3
  29.9 1.6 constant_dynamic-update-slice_fusion.2
  31.5 2.2 constant_dynamic-update-slice_fusion.1
  38.9 14.3 %reduce-scatter.3.cloned.1.call-done = f32[8,1024]{1,0:T(8,128)} async-done(((f32[32,1024]{1,0:T(8,128)}), f32[8,1024]{1,0:T(8,128)}) %reduce-scatter.3.cloned.1.call-update) | async-done | bytes 32784 | tf_op jit(solution)/shard_map/reduce_scatter | solution.py:79
  56.3 3.3 %collective-permute-done.4 = f32[8,1024]{1,0:T(8,128)S(1)} collective-permute-done((f32[8,1024]{1,0:T(8,128)S(1)}, f32[8,1024]{1,0:T(8,128)S(1)}, u32[]{:S(2)}, u32[]{:S(2)}) %collective-permute-start.4) | collective-permute-done | bytes 32800 | tf_op jit(solution)/shard_map/ppermute | solution.py:91
  62.0 3.3 %collective-permute-done.5 = f32[16,1024]{1,0:T(8,128)S(1)} collective-permute-done((f32[16,1024]{1,0:T(8,128)S(1)}, f32[16,1024]{1,0:T(8,128)S(1)}, u32[]{:S(2)}, u32[]{:S(2)}) %collective-permute-start.5) | collective-permute-done | bytes 65568 | tf_op jit(solution)/shard_map/ppermute | solution.py:91
  76.1 9.9 %convolution_bitcast_fusion.1 = f32[16,4,8,128]{3,2,1,0:T(8,128)S(1)} fusion(f32[32,16,7,128]{3,0,2,1:T(8,128)S(1)} %bitcast.198, f32[16,7,128,128]{3,2,1,0:T(8,128)} %param.11), kind=kOutput, calls=%fused_computation.7 | convolution fusion | flops 704643072 | bytes 9437184 | tf_op jit(solution)/shard_map/rtij,nrtj->nri/dot_general | solution.py:123
  87.8 2.0 collective-permute-start.10
  98.6 39.5 %all-reduce = (f32[32]{0:T(128)S(1)}, f32[32]{0:T(128)S(1)}) all-reduce(f32[32]{0:T(128)S(1)} %get-tuple-element.3, f32[32]{0:T(128)S(1)} %get-tuple-element.2), channel_id=1, replica_groups=mesh['gx'=4,'gy'=2,'gz'=4] {'gx','gy','gz'}, use_global_device_ids=true, to_apply=%region_2.3 | all-reduce | flops 64 | bytes 512 | tf_op jit(solution)/shard_map/psum | solution.py:117
  145.8 16.4 %reduce-scatter.5.cloned.1.call-done = f32[8,1024]{1,0:T(8,128)} async-done(((f32[32,1024]{1,0:T(8,128)}), f32[8,1024]{1,0:T(8,128)}) %reduce-scatter.5.cloned.1.call-update) | async-done | bytes 32784 | tf_op jit(solution)/shard_map/reduce_scatter | solution.py:79
  165.2 3.3 %collective-permute-done.14 = f32[8,1024]{1,0:T(8,128)S(1)} collective-permute-done((f32[8,1024]{1,0:T(8,128)S(1)}, f32[8,1024]{1,0:T(8,128)S(1)}, u32[]{:S(2)}, u32[]{:S(2)}) %collective-permute-start.14) | collective-permute-done | bytes 32800 | tf_op jit(solution)/shard_map/ppermute | solution.py:91
  170.8 3.4 %collective-permute-done.15 = f32[16,1024]{1,0:T(8,128)S(1)} collective-permute-done((f32[16,1024]{1,0:T(8,128)S(1)}, f32[16,1024]{1,0:T(8,128)S(1)}, u32[]{:S(2)}, u32[]{:S(2)}) %collective-permute-start.15) | collective-permute-done | bytes 65568 | tf_op jit(solution)/shard_map/ppermute | solution.py:91
  176.9 1.5 collective-permute-start.19
  184.4 40.6 %psum.30 = f32[32]{0:T(128)S(1)} all-reduce(f32[32]{0:T(128)S(1)} %multiply_reduce_fusion.1), channel_id=1, replica_groups=mesh['gx'=4,'gy'=2,'gz'=4] {'gx','gy','gz'}, use_global_device_ids=true, to_apply=%region_7.8 | all-reduce | flops 32 | bytes 256 | tf_op jit(solution)/shard_map/psum | solution.py:117
  225.9 9.9 %convolution_bitcast_fusion = f32[16,4,8,128]{3,2,1,0:T(8,128)S(1)} fusion(f32[32,16,7,128]{3,0,2,1:T(8,128)S(1)} %bitcast.197, f32[16,7,128,128]{3,2,1,0:T(8,128)} %param.11), kind=kOutput, calls=%fused_computation.6 | convolution fusion | flops 704643072 | bytes 9437184 | tf_op jit(solution)/shard_map/rtij,nrtj->nri/dot_general | solution.py:123
  236.9 2.1 collective-permute-start.21
  239.1 2.3 collective-permute-start.23
  247.5 38.2 %psum.31 = f32[32]{0:T(128)S(1)} all-reduce(f32[32]{0:T(128)S(1)} %multiply_reduce_fusion), channel_id=1, replica_groups=mesh['gx'=4,'gy'=2,'gz'=4] {'gx','gy','gz'}, use_global_device_ids=true, to_apply=%region_9.10 | all-reduce | flops 32 | bytes 256 | tf_op jit(solution)/shard_map/psum | solution.py:127
  285.8 1.9 multiply_subtract_fusion
  (222 shorter events, 69.0 us)
Async XLA Ops:
  7.2 46.1 %reduce-scatter.3.cloned.1.call-start = ((), (), s32[]{:S(2)}) async-start(), calls=%async_computation.2 | async-start | bytes 163840 | tf_op jit(solution)/shard_map/reduce_scatter | solution.py:79
  9.0 17.6 %collective-permute-start = (f32[32,128]{0,1:T(8,128)S(1)}, f32[32,128]{0,1:T(8,128)S(1)}, u32[]{:S(2)}, u32[]{:S(2)}) collective-permute-start(f32[32,128]{0,1:T(8,128)S(1)} %convolution_bitcast_fusion.7), channel_id=1, source_target_pairs={{0,1},{1,0},{2,3},{3,2},{4,5},{5,4},{6,7},{7,6},{8,9},{9,8},{10,11... | collective-permute-start | bytes 49160 | tf_op jit(solution)/shard_map/ppermute | solution.py:20
  13.1 15.1 %collective-permute-start.1 = (f32[32,128]{0,1:T(8,128)S(1)}, f32[32,128]{0,1:T(8,128)S(1)}, u32[]{:S(2)}, u32[]{:S(2)}) collective-permute-start(f32[32,128]{0,1:T(8,128)S(1)} %convolution_bitcast_fusion.6), channel_id=1, source_target_pairs={{0,2},{1,3},{2,0},{3,1},{4,6},{5,7},{6,4},{7,5},{8,10},{9,11},{10,... | collective-permute-start | bytes 49160 | tf_op jit(solution)/shard_map/ppermute | solution.py:20
  16.7 13.2 %collective-permute-start.2 = (f32[32,128]{0,1:T(8,128)S(1)}, f32[32,128]{0,1:T(8,128)S(1)}, u32[]{:S(2)}, u32[]{:S(2)}) collective-permute-start(f32[32,128]{0,1:T(8,128)S(1)} %convolution_bitcast_fusion.5), channel_id=1, source_target_pairs={{0,4},{1,5},{2,6},{3,7},{4,0},{5,1},{6,2},{7,3},{8,12},{9,13},{10,... | collective-permute-start | bytes 49160 | tf_op jit(solution)/shard_map/ppermute | solution.py:20
  17.7 13.8 %collective-permute-start.3 = (f32[32,128]{0,1:T(8,128)S(1)}, f32[32,128]{0,1:T(8,128)S(1)}, u32[]{:S(2)}, u32[]{:S(2)}) collective-permute-start(f32[32,128]{0,1:T(8,128)S(1)} %convolution_bitcast_fusion.4), channel_id=1, source_target_pairs={{0,8},{1,9},{2,10},{3,11},{4,12},{5,13},{6,14},{7,15},{8,0},{9,1},... | collective-permute-start | bytes 49160 | tf_op jit(solution)/shard_map/ppermute | solution.py:20
  36.6 125.5 %reduce-scatter.5.cloned.1.call-start = ((), (), s32[]{:S(2)}) async-start(), calls=%async_computation.3 | async-start | bytes 163840 | tf_op jit(solution)/shard_map/reduce_scatter | solution.py:79
  55.6 4.0 %collective-permute-start.4 = (f32[8,1024]{1,0:T(8,128)S(1)}, f32[8,1024]{1,0:T(8,128)S(1)}, u32[]{:S(2)}, u32[]{:S(2)}) collective-permute-start(f32[8,1024]{1,0:T(8,128)S(1)} %reshape.579), channel_id=1, source_target_pairs={{0,1},{1,0},{2,3},{3,2},{4,5},{5,4},{6,7},{7,6},{8,9},{9,8},{10,11... | collective-permute-start | bytes 98312 | tf_op jit(solution)/shard_map/ppermute | solution.py:91
  59.7 5.7 %collective-permute-start.5 = (f32[16,1024]{1,0:T(8,128)S(1)}, f32[16,1024]{1,0:T(8,128)S(1)}, u32[]{:S(2)}, u32[]{:S(2)}) collective-permute-start(f32[16,1024]{1,0:T(8,128)S(1)} %maximum_select_fusion.4), channel_id=1, source_target_pairs={{0,2},{1,3},{2,0},{3,1},{4,6},{5,7},{6,4},{7,5},{8,10},{9,11},{10,... | collective-permute-start | bytes 196616 | tf_op jit(solution)/shard_map/ppermute | solution.py:91
  68.0 4.7 %collective-permute-start.7 = (f32[32,128]{1,0:T(8,128)S(1)}, f32[32,128]{1,0:T(8,128)S(1)}, u32[]{:S(2)}, u32[]{:S(2)}) collective-permute-start(f32[32,128]{1,0:T(8,128)S(1)} %fusion.61), channel_id=1, source_target_pairs={{0,2},{1,3},{2,0},{3,1},{4,6},{5,7},{6,4},{7,5},{8,10},{9,11},{10,... | collective-permute-start | bytes 49160 | tf_op jit(solution)/shard_map/ppermute | solution.py:20
  68.6 5.0 %collective-permute-start.8 = (f32[32,128]{1,0:T(8,128)S(1)}, f32[32,128]{1,0:T(8,128)S(1)}, u32[]{:S(2)}, u32[]{:S(2)}) collective-permute-start(f32[32,128]{1,0:T(8,128)S(1)} %fusion.57), channel_id=1, source_target_pairs={{0,4},{1,5},{2,6},{3,7},{4,0},{5,1},{6,2},{7,3},{8,12},{9,13},{10,... | collective-permute-start | bytes 49160 | tf_op jit(solution)/shard_map/ppermute | solution.py:20
  68.6 5.8 %collective-permute-start.9 = (f32[32,128]{1,0:T(8,128)S(1)}, f32[32,128]{1,0:T(8,128)S(1)}, u32[]{:S(2)}, u32[]{:S(2)}) collective-permute-start(f32[32,128]{1,0:T(8,128)S(1)} %fusion.53), channel_id=1, source_target_pairs={{0,8},{1,9},{2,10},{3,11},{4,12},{5,13},{6,14},{7,15},{8,0},{9,1},... | collective-permute-start | bytes 49160 | tf_op jit(solution)/shard_map/ppermute | solution.py:20
  87.8 6.4 %collective-permute-start.10 = (f32[32,128]{1,0:T(8,128)S(1)}, f32[32,128]{1,0:T(8,128)S(1)}, u32[]{:S(2)}, u32[]{:S(2)}) collective-permute-start(f32[32,128]{1,0:T(8,128)S(1)} %fusion.64), channel_id=1, source_target_pairs={{0,1},{1,0},{2,3},{3,2},{4,5},{5,4},{6,7},{7,6},{8,9},{9,8},{10,11... | collective-permute-start | bytes 49160 | tf_op jit(solution)/shard_map/ppermute | solution.py:20
  89.9 5.2 %collective-permute-start.11 = (f32[32,128]{1,0:T(8,128)S(1)}, f32[32,128]{1,0:T(8,128)S(1)}, u32[]{:S(2)}, u32[]{:S(2)}) collective-permute-start(f32[32,128]{1,0:T(8,128)S(1)} %fusion.60), channel_id=1, source_target_pairs={{0,2},{1,3},{2,0},{3,1},{4,6},{5,7},{6,4},{7,5},{8,10},{9,11},{10,... | collective-permute-start | bytes 49160 | tf_op jit(solution)/shard_map/ppermute | solution.py:20
  90.4 5.7 %collective-permute-start.12 = (f32[32,128]{1,0:T(8,128)S(1)}, f32[32,128]{1,0:T(8,128)S(1)}, u32[]{:S(2)}, u32[]{:S(2)}) collective-permute-start(f32[32,128]{1,0:T(8,128)S(1)} %fusion.56), channel_id=1, source_target_pairs={{0,4},{1,5},{2,6},{3,7},{4,0},{5,1},{6,2},{7,3},{8,12},{9,13},{10,... | collective-permute-start | bytes 49160 | tf_op jit(solution)/shard_map/ppermute | solution.py:20
  90.4 7.1 %collective-permute-start.13 = (f32[32,128]{1,0:T(8,128)S(1)}, f32[32,128]{1,0:T(8,128)S(1)}, u32[]{:S(2)}, u32[]{:S(2)}) collective-permute-start(f32[32,128]{1,0:T(8,128)S(1)} %fusion.52), channel_id=1, source_target_pairs={{0,8},{1,9},{2,10},{3,11},{4,12},{5,13},{6,14},{7,15},{8,0},{9,1},... | collective-permute-start | bytes 49160 | tf_op jit(solution)/shard_map/ppermute | solution.py:20
  164.5 4.0 %collective-permute-start.14 = (f32[8,1024]{1,0:T(8,128)S(1)}, f32[8,1024]{1,0:T(8,128)S(1)}, u32[]{:S(2)}, u32[]{:S(2)}) collective-permute-start(f32[8,1024]{1,0:T(8,128)S(1)} %reshape.587), channel_id=1, source_target_pairs={{0,1},{1,0},{2,3},{3,2},{4,5},{5,4},{6,7},{7,6},{8,9},{9,8},{10,11... | collective-permute-start | bytes 98312 | tf_op jit(solution)/shard_map/ppermute | solution.py:91
  168.5 5.7 %collective-permute-start.15 = (f32[16,1024]{1,0:T(8,128)S(1)}, f32[16,1024]{1,0:T(8,128)S(1)}, u32[]{:S(2)}, u32[]{:S(2)}) collective-permute-start(f32[16,1024]{1,0:T(8,128)S(1)} %maximum_select_fusion.5), channel_id=1, source_target_pairs={{0,2},{1,3},{2,0},{3,1},{4,6},{5,7},{6,4},{7,5},{8,10},{9,11},{10,... | collective-permute-start | bytes 196616 | tf_op jit(solution)/shard_map/ppermute | solution.py:91
  176.2 4.7 %collective-permute-start.17 = (f32[32,128]{1,0:T(8,128)S(1)}, f32[32,128]{1,0:T(8,128)S(1)}, u32[]{:S(2)}, u32[]{:S(2)}) collective-permute-start(f32[32,128]{1,0:T(8,128)S(1)} %fusion.59), channel_id=1, source_target_pairs={{0,2},{1,3},{2,0},{3,1},{4,6},{5,7},{6,4},{7,5},{8,10},{9,11},{10,... | collective-permute-start | bytes 49160 | tf_op jit(solution)/shard_map/ppermute | solution.py:20
  176.9 5.0 %collective-permute-start.18 = (f32[32,128]{1,0:T(8,128)S(1)}, f32[32,128]{1,0:T(8,128)S(1)}, u32[]{:S(2)}, u32[]{:S(2)}) collective-permute-start(f32[32,128]{1,0:T(8,128)S(1)} %fusion.55), channel_id=1, source_target_pairs={{0,4},{1,5},{2,6},{3,7},{4,0},{5,1},{6,2},{7,3},{8,12},{9,13},{10,... | collective-permute-start | bytes 49160 | tf_op jit(solution)/shard_map/ppermute | solution.py:20
  176.9 5.8 %collective-permute-start.19 = (f32[32,128]{1,0:T(8,128)S(1)}, f32[32,128]{1,0:T(8,128)S(1)}, u32[]{:S(2)}, u32[]{:S(2)}) collective-permute-start(f32[32,128]{1,0:T(8,128)S(1)} %fusion.51), channel_id=1, source_target_pairs={{0,8},{1,9},{2,10},{3,11},{4,12},{5,13},{6,14},{7,15},{8,0},{9,1},... | collective-permute-start | bytes 49160 | tf_op jit(solution)/shard_map/ppermute | solution.py:20
  236.9 6.3 %collective-permute-start.20 = (f32[32,128]{1,0:T(8,128)S(1)}, f32[32,128]{1,0:T(8,128)S(1)}, u32[]{:S(2)}, u32[]{:S(2)}) collective-permute-start(f32[32,128]{1,0:T(8,128)S(1)} %fusion.62), channel_id=1, source_target_pairs={{0,1},{1,0},{2,3},{3,2},{4,5},{5,4},{6,7},{7,6},{8,9},{9,8},{10,11... | collective-permute-start | bytes 49160 | tf_op jit(solution)/shard_map/ppermute | solution.py:20
  236.9 7.0 %collective-permute-start.21 = (f32[32,128]{1,0:T(8,128)S(1)}, f32[32,128]{1,0:T(8,128)S(1)}, u32[]{:S(2)}, u32[]{:S(2)}) collective-permute-start(f32[32,128]{1,0:T(8,128)S(1)} %fusion.58), channel_id=1, source_target_pairs={{0,2},{1,3},{2,0},{3,1},{4,6},{5,7},{6,4},{7,5},{8,10},{9,11},{10,... | collective-permute-start | bytes 49160 | tf_op jit(solution)/shard_map/ppermute | solution.py:20
  239.1 5.8 %collective-permute-start.22 = (f32[32,128]{1,0:T(8,128)S(1)}, f32[32,128]{1,0:T(8,128)S(1)}, u32[]{:S(2)}, u32[]{:S(2)}) collective-permute-start(f32[32,128]{1,0:T(8,128)S(1)} %fusion.54), channel_id=1, source_target_pairs={{0,4},{1,5},{2,6},{3,7},{4,0},{5,1},{6,2},{7,3},{8,12},{9,13},{10,... | collective-permute-start | bytes 49160 | tf_op jit(solution)/shard_map/ppermute | solution.py:20
  239.1 6.7 %collective-permute-start.23 = (f32[32,128]{1,0:T(8,128)S(1)}, f32[32,128]{1,0:T(8,128)S(1)}, u32[]{:S(2)}, u32[]{:S(2)}) collective-permute-start(f32[32,128]{1,0:T(8,128)S(1)} %fusion.50), channel_id=1, source_target_pairs={{0,8},{1,9},{2,10},{3,11},{4,12},{5,13},{6,14},{7,15},{8,0},{9,1},... | collective-permute-start | bytes 49160 | tf_op jit(solution)/shard_map/ppermute | solution.py:20
  (32 other events, 735.8 us)
Sparse Core Ops, SparseCore 0:
  36.7 16.4 reduce-scatter.2
  142.3 19.8 reduce-scatter.4
